TPU v7x, 32 devices: a whole 2x2x4 slice. The times are simulated.
32 devices in a mesh: lat: 4 (over y, x), lon: 8 (over z, core).
Axes of the slice: x: 2, y: 2, z: 4, core: 2. Of those that a mesh axis runs over, the one named last changes fastest.
Arguments:
- fine_map: bfloat16 [4, 48, 256, 400], P(None, 'lat', 'lon'), may hold values from -26 to 26
- ocean_mask: int32 [4, 48, 256], P(None, 'lat', 'lon'), may hold values from 0 to 1
- out_grad: bfloat16 [4, 48, 256, 400], P(None, 'lat', 'lon'), may hold values from -6 to 6
- encode_depth: bfloat16 [7, 7, 400], replicated, may hold values from -0.875 to 0.875
- encode_gain: bfloat16 [400], replicated, may hold values from 0.099609375 to 1.8984375
- encode_shift: bfloat16 [400], replicated, may hold values from -3 to 3
- encode_up: bfloat16 [400, 1600], P('lat'), may hold values from -0.3125 to 0.3125
- encode_up_bias: bfloat16 [1600], replicated, may hold values from -3 to 3
- encode_down: bfloat16 [1600, 400], P('lat'), may hold values from -0.15625 to 0.15625
- encode_down_bias: bfloat16 [400], replicated, may hold values from -3 to 3
- widen_weight: bfloat16 [400, 800], P('lat'), may hold values from -0.3125 to 0.3125
- widen_bias: bfloat16 [800], replicated, may hold values from -3 to 3
- bottle_depth: bfloat16 [7, 7, 800], replicated, may hold values from -0.875 to 0.875
- bottle_gain: bfloat16 [800], replicated, may hold values from 0.099609375 to 1.8984375
- bottle_shift: bfloat16 [800], replicated, may hold values from -3 to 3
- bottle_up: bfloat16 [800, 3200], P('lat'), may hold values from -0.21875 to 0.21875
- bottle_up_bias: bfloat16 [3200], replicated, may hold values from -3 to 3
- bottle_down: bfloat16 [3200, 800], P('lat'), may hold values from -0.109375 to 0.109375
- bottle_down_bias: bfloat16 [800], replicated, may hold values from -3 to 3
- merge_weight: bfloat16 [1200, 400], P('lat'), may hold values from -0.1875 to 0.1875
- merge_bias: bfloat16 [400], replicated, may hold values from -3 to 3
- decode_depth: bfloat16 [7, 7, 400], replicated, may hold values from -0.875 to 0.875
- decode_gain: bfloat16 [400], replicated, may hold values from 0.099609375 to 1.8984375
- decode_shift: bfloat16 [400], replicated, may hold values from -3 to 3
- decode_up: bfloat16 [400, 1600], P('lat'), may hold values from -0.3125 to 0.3125
- decode_up_bias: bfloat16 [1600], replicated, may hold values from -3 to 3
- decode_down: bfloat16 [1600, 400], P('lat'), may hold values from -0.15625 to 0.15625
- decode_down_bias: bfloat16 [400], replicated, may hold values from -3 to 3
Outputs:
- result: bfloat16 [4, 48, 256, 400], P(None, 'lat', 'lon')
- fine_grad: bfloat16 [4, 48, 256, 400], P(None, 'lat', 'lon')
- encode_depth_grad: float32 [7, 7, 400], replicated
- encode_gain_grad: float32 [400], replicated
- encode_shift_grad: float32 [400], replicated
- encode_up_grad: float32 [400, 1600], replicated
- encode_up_bias_grad: float32 [1600], replicated
- encode_down_grad: float32 [1600, 400], replicated
- encode_down_bias_grad: float32 [400], replicated
- widen_weight_grad: float32 [400, 800], replicated
- widen_bias_grad: float32 [800], replicated
- bottle_depth_grad: float32 [7, 7, 800], replicated
- bottle_gain_grad: float32 [800], replicated
- bottle_shift_grad: float32 [800], replicated
- bottle_up_grad: float32 [800, 3200], replicated
- bottle_up_bias_grad: float32 [3200], replicated
- bottle_down_grad: float32 [3200, 800], replicated
- bottle_down_bias_grad: float32 [800], replicated
- merge_weight_grad: float32 [1200, 400], replicated
- merge_bias_grad: float32 [400], replicated
- decode_depth_grad: float32 [7, 7, 400], replicated
- decode_gain_grad: float32 [400], replicated
- decode_shift_grad: float32 [400], replicated
- decode_up_grad: float32 [400, 1600], replicated
- decode_up_bias_grad: float32 [1600], replicated
- decode_down_grad: float32 [1600, 400], replicated
- decode_down_bias_grad: float32 [400], replicated
All inputs are finite; a program needn't handle non-finite values.
Results may differ from a plain program's by a relative error of at most 0.018.
Values may be sent and summed in bfloat16 or wider, within the bound.
No kernel may reach another device: no remote copies, remote signals or barrier semaphores. Data moves between devices by JAX's collectives and lax.ppermute only.
A program may use at most 320 MiB of HBM per device.

v0:
```python
import math
import jax
import jax.numpy as jnp
from jax import lax
from jax.sharding import PartitionSpec as P

epsilon = 1e-05


def padded(block, sides, width, periodic):
    for axis, dim in sides:
        count = lax.axis_size(axis)
        forward = [(i, i + 1) for i in range(count - 1)]
        if periodic:
            forward.append((count - 1, 0))
        backward = [(target, source) for source, target in forward]
        low = lax.ppermute(
            lax.slice_in_dim(block, block.shape[dim] - width, None, axis=dim), axis, forward
        )
        high = lax.ppermute(lax.slice_in_dim(block, 0, width, axis=dim), axis, backward)
        block = jnp.concatenate([low, block, high], axis=dim)
    return block


def widen_map(source):
    wrapped = padded(source, (("lon", 2),), 3, True)
    return padded(wrapped, (("lat", 1),), 3, False)


def stencil(extended, kernel, height, breadth):
    taps = kernel.astype(jnp.float32)
    summed = jnp.zeros((extended.shape[0], height, breadth, extended.shape[3]), jnp.float32)
    for across in range(7):
        for column in range(7):
            summed = summed + taps[across, column] * extended[
                :, across : across + height, column : column + breadth, :
            ].astype(jnp.float32)
    return summed


def kernel_terms(extended, grad_mixed, height, breadth):
    upstream = grad_mixed.astype(jnp.float32)
    all_rows = []
    for across in range(7):
        row_terms = []
        for column in range(7):
            window = extended[:, across : across + height, column : column + breadth, :].astype(
                jnp.float32
            )
            row_terms.append(jnp.sum(window * upstream, axis=(0, 1, 2)))
        all_rows.append(jnp.stack(row_terms))
    return jnp.stack(all_rows)


def cross_rows(former, latter):
    return lax.dot_general(
        former, latter, (((0,), (0,)), ((), ())), preferred_element_type=jnp.float32
    )


def by_transpose(former, latter):
    return lax.dot_general(
        former, latter, (((1,), (1,)), ((), ())), preferred_element_type=jnp.float32
    )


def exact_gelu(values):
    return jax.nn.gelu(values, approximate=False)


def block_forward(source, params, sea_mask):
    kernel, scale_gain, norm_shift, up_weight, up_bias, down_weight, down_bias = params
    date_count, height, breadth, channels = source.shape
    extended = widen_map(source)
    mixed = stencil(extended, kernel, height, breadth)
    local_sums = (
        jnp.sum(sea_mask * mixed, axis=(0, 1, 2)),
        jnp.sum(sea_mask * mixed * mixed, axis=(0, 1, 2)),
        jnp.sum(sea_mask),
    )
    first_sum, square_sum, ocean_count = lax.psum(
        (local_sums[0], local_sums[1], local_sums[2]), ("lat", "lon")
    )
    mean_value = first_sum / ocean_count
    norm_factor = lax.rsqrt(square_sum / ocean_count - mean_value * mean_value + epsilon)
    unit_norm = (mixed - mean_value) * norm_factor
    normed = (
        (unit_norm * scale_gain.astype(jnp.float32) + norm_shift.astype(jnp.float32))
        .astype(jnp.bfloat16)
        .reshape(-1, channels)
    )
    hidden = jnp.dot(normed, up_weight, preferred_element_type=jnp.float32) + up_bias.astype(
        jnp.float32
    )
    active = exact_gelu(hidden).astype(jnp.bfloat16)
    branch = jnp.dot(active, down_weight, preferred_element_type=jnp.float32) + down_bias.astype(
        jnp.float32
    )
    output = sea_mask * (source.astype(jnp.float32) + branch.reshape(source.shape))
    stored = (extended, unit_norm, norm_factor, ocean_count, normed, hidden, active)
    return (output, stored)


def block_backward(grad_output, params, sea_mask, stored):
    kernel, scale_gain, norm_shift, up_weight, up_bias, down_weight, down_bias = params
    extended, unit_norm, norm_factor, ocean_count, normed, hidden_store, active = stored
    date_count, height, breadth, channels = unit_norm.shape
    grad_branch = (sea_mask * grad_output).astype(jnp.bfloat16).reshape(-1, channels)
    grad_down = cross_rows(active, grad_branch)
    grad_down_bias = jnp.sum(grad_branch.astype(jnp.float32), axis=0)
    grad_active = by_transpose(grad_branch, down_weight)
    unused_value, gelu_back = jax.vjp(exact_gelu, hidden_store)
    grad_hidden = gelu_back(grad_active)[0].astype(jnp.bfloat16)
    grad_up = cross_rows(normed, grad_hidden)
    grad_up_bias = jnp.sum(grad_hidden.astype(jnp.float32), axis=0)
    grad_normed = by_transpose(grad_hidden, up_weight).reshape(unit_norm.shape)
    local_back = (
        jnp.sum(grad_normed, axis=(0, 1, 2)),
        jnp.sum(grad_normed * unit_norm, axis=(0, 1, 2)),
    )
    grad_shift, grad_gain = lax.psum((local_back[0], local_back[1]), ("lat", "lon"))
    gain_float = scale_gain.astype(jnp.float32)
    grad_mixed = norm_factor * (
        gain_float * grad_normed
        - sea_mask / ocean_count * (gain_float * grad_shift + unit_norm * (gain_float * grad_gain))
    )
    grad_mixed = grad_mixed.astype(jnp.bfloat16)
    grad_extended = widen_map(grad_mixed)
    grad_source = sea_mask * grad_output + stencil(
        grad_extended, kernel[::-1, ::-1], height, breadth
    )
    grad_kernel = kernel_terms(extended, grad_mixed, height, breadth)
    return (
        grad_source,
        (grad_kernel, grad_gain, grad_shift, grad_up, grad_up_bias, grad_down, grad_down_bias),
    )


def unpack(vector, extents):
    pieces = []
    offset = 0
    for extent in extents:
        length = math.prod(extent)
        pieces.append(vector[offset : offset + length].reshape(extent))
        offset = offset + length
    return pieces


def shards(
    fine_map,
    ocean_mask,
    out_grad,
    encode_depth,
    encode_gain,
    encode_shift,
    encode_up,
    encode_up_bias,
    encode_down,
    encode_down_bias,
    widen_weight,
    widen_bias,
    bottle_depth,
    bottle_gain,
    bottle_shift,
    bottle_up,
    bottle_up_bias,
    bottle_down,
    bottle_down_bias,
    merge_weight,
    merge_bias,
    decode_depth,
    decode_gain,
    decode_shift,
    decode_up,
    decode_up_bias,
    decode_down,
    decode_down_bias,
):
    (
        encode_up,
        encode_down,
        widen_weight,
        bottle_up,
        bottle_down,
        merge_weight,
        decode_up,
        decode_down,
    ) = (
        lax.all_gather(encode_up, "lat", axis=0, tiled=True),
        lax.all_gather(encode_down, "lat", axis=0, tiled=True),
        lax.all_gather(widen_weight, "lat", axis=0, tiled=True),
        lax.all_gather(bottle_up, "lat", axis=0, tiled=True),
        lax.all_gather(bottle_down, "lat", axis=0, tiled=True),
        lax.all_gather(merge_weight, "lat", axis=0, tiled=True),
        lax.all_gather(decode_up, "lat", axis=0, tiled=True),
        lax.all_gather(decode_down, "lat", axis=0, tiled=True),
    )
    date_count, height, breadth, channels = fine_map.shape
    half_height, half_breadth = (height // 2, breadth // 2)
    wide_channels = widen_weight.shape[1]
    sea_fine = ocean_mask.astype(jnp.float32)[..., None]
    sea_coarse = jnp.max(
        sea_fine.reshape(date_count, half_height, 2, half_breadth, 2, 1), axis=(2, 4)
    )
    encode = (
        encode_depth,
        encode_gain,
        encode_shift,
        encode_up,
        encode_up_bias,
        encode_down,
        encode_down_bias,
    )
    bottle = (
        bottle_depth,
        bottle_gain,
        bottle_shift,
        bottle_up,
        bottle_up_bias,
        bottle_down,
        bottle_down_bias,
    )
    decode = (
        decode_depth,
        decode_gain,
        decode_shift,
        decode_up,
        decode_up_bias,
        decode_down,
        decode_down_bias,
    )
    merge_upper = merge_weight[:wide_channels]
    merge_lower = merge_weight[wide_channels:]
    encode_out, encode_stored = block_forward(fine_map, encode, sea_fine)
    skip_map = encode_out.astype(jnp.bfloat16)
    skip_rows = skip_map.reshape(-1, channels)
    blocks_fine = skip_map.reshape(date_count, half_height, 2, half_breadth, 2, channels).astype(
        jnp.float32
    )
    pooled = (jnp.sum(blocks_fine, axis=(2, 4)) * 0.25).astype(jnp.bfloat16).reshape(-1, channels)
    coarse_in = jnp.dot(
        pooled, widen_weight, preferred_element_type=jnp.float32
    ) + widen_bias.astype(jnp.float32)
    coarse_in = coarse_in.astype(jnp.bfloat16).reshape(
        date_count, half_height, half_breadth, wide_channels
    )
    coarse_out, coarse_stored = block_forward(coarse_in, bottle, sea_coarse)
    coarse_low = coarse_out.astype(jnp.bfloat16).reshape(-1, wide_channels)
    upper_part = jnp.dot(coarse_low, merge_upper, preferred_element_type=jnp.float32)
    upper_part = upper_part.reshape(date_count, half_height, 1, half_breadth, 1, channels)
    lower_part = jnp.dot(skip_rows, merge_lower, preferred_element_type=jnp.float32)
    lower_part = lower_part.reshape(date_count, half_height, 2, half_breadth, 2, channels)
    merged = (lower_part + upper_part).reshape(
        date_count, height, breadth, channels
    ) + merge_bias.astype(jnp.float32)
    decode_in = merged.astype(jnp.bfloat16)
    decode_out, decode_stored = block_forward(decode_in, decode, sea_fine)
    result = decode_out.astype(jnp.bfloat16)
    grad_decode_in, decode_grads = block_backward(
        out_grad.astype(jnp.float32), decode, sea_fine, decode_stored
    )
    grad_merged = grad_decode_in.astype(jnp.bfloat16).reshape(-1, channels)
    coarse_grid = coarse_low.reshape(date_count, half_height, 1, half_breadth, 1, wide_channels)
    upsampled_rows = jnp.broadcast_to(
        coarse_grid, (date_count, half_height, 2, half_breadth, 2, wide_channels)
    ).reshape(-1, wide_channels)
    grad_merge_weight = jnp.concatenate(
        [cross_rows(upsampled_rows, grad_merged), cross_rows(skip_rows, grad_merged)], axis=0
    )
    grad_merge_bias = jnp.sum(grad_merged.astype(jnp.float32), axis=0)
    grad_upsampled = by_transpose(grad_merged, merge_upper)
    grad_coarse = jnp.sum(
        grad_upsampled.reshape(date_count, half_height, 2, half_breadth, 2, wide_channels),
        axis=(2, 4),
    )
    grad_skip_direct = by_transpose(grad_merged, merge_lower)
    grad_coarse_in, bottle_grads = block_backward(grad_coarse, bottle, sea_coarse, coarse_stored)
    grad_wide = grad_coarse_in.astype(jnp.bfloat16).reshape(-1, wide_channels)
    grad_widen_weight = cross_rows(pooled, grad_wide)
    grad_widen_bias = jnp.sum(grad_wide.astype(jnp.float32), axis=0)
    grad_pooled = (
        by_transpose(grad_wide, widen_weight).reshape(
            date_count, half_height, 1, half_breadth, 1, channels
        )
        * 0.25
    )
    grad_skip = (
        grad_skip_direct.reshape(date_count, half_height, 2, half_breadth, 2, channels)
        + grad_pooled
    )
    grad_skip = grad_skip.reshape(date_count, height, breadth, channels)
    grad_fine, encode_grads = block_backward(grad_skip, encode, sea_fine, encode_stored)
    fine_grad = grad_fine.astype(jnp.bfloat16)
    large_parts = [
        encode_grads[3],
        encode_grads[5],
        grad_widen_weight,
        bottle_grads[3],
        bottle_grads[5],
        grad_merge_weight,
        decode_grads[3],
        decode_grads[5],
    ]
    large_extents = [part_grad.shape for part_grad in large_parts]
    large_vector = jnp.concatenate([part_grad.reshape(-1) for part_grad in large_parts])
    share = lax.psum_scatter(large_vector, ("lat", "lon"), scatter_dimension=0, tiled=True)
    large_total = lax.all_gather(
        share.astype(jnp.bfloat16), ("lat", "lon"), axis=0, tiled=True
    ).astype(share.dtype)
    small_parts = [
        encode_grads[0],
        encode_grads[4],
        encode_grads[6],
        grad_widen_bias,
        bottle_grads[0],
        bottle_grads[4],
        bottle_grads[6],
        grad_merge_bias,
        decode_grads[0],
        decode_grads[4],
        decode_grads[6],
    ]
    small_extents = [part_grad.shape for part_grad in small_parts]
    small_vector = jnp.concatenate([part_grad.reshape(-1) for part_grad in small_parts])
    small_total = lax.psum(small_vector, ("lat", "lon"))
    (
        encode_up_sum,
        encode_down_sum,
        widen_w_sum,
        bottle_up_sum,
        bottle_down_sum,
        merge_w_sum,
        decode_up_sum,
        decode_down_sum,
    ) = unpack(large_total, large_extents)
    (
        encode_kernel_sum,
        encode_upb_sum,
        encode_downb_sum,
        widen_b_sum,
        bottle_kernel_sum,
        bottle_upb_sum,
        bottle_downb_sum,
        merge_b_sum,
        decode_kernel_sum,
        decode_upb_sum,
        decode_downb_sum,
    ) = unpack(small_total, small_extents)
    return (
        result,
        fine_grad,
        encode_kernel_sum,
        encode_grads[1],
        encode_grads[2],
        encode_up_sum,
        encode_upb_sum,
        encode_down_sum,
        encode_downb_sum,
        widen_w_sum,
        widen_b_sum,
        bottle_kernel_sum,
        bottle_grads[1],
        bottle_grads[2],
        bottle_up_sum,
        bottle_upb_sum,
        bottle_down_sum,
        bottle_downb_sum,
        merge_w_sum,
        merge_b_sum,
        decode_kernel_sum,
        decode_grads[1],
        decode_grads[2],
        decode_up_sum,
        decode_upb_sum,
        decode_down_sum,
        decode_downb_sum,
    )


def solution(mesh):
    placed = (
        P(None, "lat", "lon", None),
        P(None, "lat", "lon"),
        P(None, "lat", "lon", None),
        P(),
        P(),
        P(),
        P("lat", None),
        P(),
        P("lat", None),
        P(),
        P("lat", None),
        P(),
        P(),
        P(),
        P(),
        P("lat", None),
        P(),
        P("lat", None),
        P(),
        P("lat", None),
        P(),
        P(),
        P(),
        P(),
        P("lat", None),
        P(),
        P("lat", None),
        P(),
    )
    return jax.shard_map(
        shards,
        mesh=mesh,
        in_specs=placed,
        out_specs=(
            P(None, "lat", "lon", None),
            P(None, "lat", "lon", None),
            P(),
            P(),
            P(),
            P(),
            P(),
            P(),
            P(),
            P(),
            P(),
            P(),
            P(),
            P(),
            P(),
            P(),
            P(),
            P(),
            P(),
            P(),
            P(),
            P(),
            P(),
            P(),
            P(),
            P(),
            P(),
        ),
        check_vma=False,
    )
```

profile of v0, /device:TPU:0, one launch (start us, length us, event | category | flops | bytes accessed | tf_op | source)
XLA Modules:
  0.0 2301.6 jit_solution(13207212915180531190)
XLA Ops:
  32.2 21.0 all-gather.1
  53.2 15.3 all-gather.2
  125.6 26.5 %multiply_reduce_fusion.1 = (f32[400]{0:T(512)}, f32[400]{0:T(512)}, f32[4,12,32,400]{3,2,1,0:T(8,128)}) fusion(f32[4,12,32]{2,1,0:T(8,128)S(1)} %copy-done.50, bf16[4,15,38,400]{3,2,1,0:T(8,128)(2,1)S(1)} %get-tuple-element.441, f32[400]{0:T(512)} %bitcast.523, f32[400]{0:T(512)} %bitcast.522, f32[400]{0:T(512)} %bitcast.521, f32[400]{0:T(512)} %bitcast.520, ...), kind=kLoop, calls=%fused_computation.214 | loop fusion | flops 97688800 | bytes 59185344 | tf_op jit(solution)/shard_map/reduce_sum | solution.py:77
  152.1 43.1 %all-reduce.7 = (f32[400]{0:T(512)S(1)}, f32[]{:T(128)}, f32[400]{0:T(512)S(1)}) all-reduce(f32[400]{0:T(512)} %get-tuple-element.207, f32[]{:T(128)} %convert_reduce_fusion.9, f32[400]{0:T(512)} %get-tuple-element.206), channel_id=1, replica_groups=mesh['lat'=4,'lon'=8] {'lat','lon'}, use_global_device_ids=true, to_apply=%region_5.0 | all-reduce | flops 801 | bytes 6408 | tf_op jit(solution)/shard_map/psum | solution.py:81
  201.4 29.4 %multiply_convert_fusion.1 = (bf16[1536,1600]{0,1:T(8,128)(2,1)}, f32[1536,1600]{0,1:T(8,128)}, f32[1536,1600]{0,1:T(8,128)}) fusion(f32[1600]{0:T(1024)S(1)} %copy-done.321, bf16[1536,400]{1,0:T(8,128)(2,1)S(1)} %bitcast.461, bf16[400,1600]{1,0:T(8,128)(2,1)} %reshape.643), kind=kOutput, calls=%fused_computation.171 | convolution fusion | flops 2128281600 | bytes 27091200 | tf_op jit(solution)/shard_map/dot_general | solution.py:92
  269.2 12.5 collective-permute-done.6
  281.7 18.0 collective-permute-done.7
  313.0 39.1 %all-reduce.6 = (f32[800]{0:T(1024)S(1)}, f32[]{:T(128)}, f32[800]{0:T(1024)S(1)}) all-reduce(f32[800]{0:T(1024)S(1)} %get-tuple-element.279, f32[]{:T(128)} %reduce_sum.1550, f32[800]{0:T(1024)S(1)} %get-tuple-element.278), channel_id=1, replica_groups=mesh['lat'=4,'lon'=8] {'lat','lon'}, use_global_device_ids=true, to_apply=%region_13.0 | all-reduce | flops 1601 | bytes 12808 | tf_op jit(solution)/shard_map/psum | solution.py:81
  353.1 16.4 multiply_convert_fusion.2
  407.7 12.8 collective-permute-done.11
  425.0 24.8 %multiply_reduce_fusion = (f32[400]{0:T(512)S(1)}, f32[400]{0:T(512)S(1)}, f32[4,12,32,400]{3,2,1,0:T(8,128)}) fusion(f32[4,12,32]{2,1,0:T(8,128)S(1)} %copy-done.52, bf16[4,15,38,400]{3,2,1,0:T(8,128)(2,1)S(1)} %get-tuple-element.437, f32[400]{0:T(512)} %bitcast.594, f32[400]{0:T(512)} %bitcast.593, f32[400]{0:T(512)} %bitcast.592, f32[400]{0:T(512)} %bitcast.591, ...), kind=kLoop, calls=%fused_computation.212 | loop fusion | flops 103218400 | bytes 55614144 | tf_op jit(solution)/shard_map/reduce_sum | solution.py:77
  449.9 38.6 %all-reduce.5 = (f32[400]{0:T(512)S(1)}, f32[400]{0:T(512)S(1)}) all-reduce(f32[400]{0:T(512)S(1)} %get-tuple-element.205, f32[400]{0:T(512)S(1)} %get-tuple-element.204), channel_id=1, replica_groups=mesh['lat'=4,'lon'=8] {'lat','lon'}, use_global_device_ids=true, to_apply=%region_17.0 | all-reduce | flops 800 | bytes 6400 | tf_op jit(solution)/shard_map/psum | solution.py:81
  492.8 30.1 %multiply_convert_fusion = (bf16[1536,1600]{0,1:T(8,128)(2,1)}, f32[1536,1600]{0,1:T(8,128)}, f32[1536,1600]{0,1:T(8,128)}) fusion(f32[1600]{0:T(1024)S(1)} %copy-done.320, bf16[1536,400]{1,0:T(8,128)(2,1)S(1)} %bitcast.463, bf16[400,1600]{1,0:T(8,128)(2,1)S(1)} %copy-done.62), kind=kOutput, calls=%fused_computation.158 | convolution fusion | flops 2128281600 | bytes 27091200 | tf_op jit(solution)/shard_map/dot_general | solution.py:92
  522.9 12.3 convert_reduce_fusion
  550.6 41.1 %all-reduce.4 = (f32[400]{0:T(512)S(1)}, f32[400]{0:T(512)S(1)}) all-reduce(f32[400]{0:T(512)S(1)} %multiply_reduce_fusion.3, f32[400]{0:T(512)S(1)} %get-tuple-element.689), channel_id=1, replica_groups=mesh['lat'=4,'lon'=8] {'lat','lon'}, use_global_device_ids=true, to_apply=%region_21.0 | all-reduce | flops 800 | bytes 6400 | tf_op jit(solution)/shard_map/psum | solution.py:121
  591.7 23.0 %fusion.193 = (f32[400]{0:T(512)S(1)}, f32[400]{0:T(512)S(1)}, f32[400]{0:T(512)S(1)}, f32[400]{0:T(512)S(1)}, f32[400]{0:T(512)S(1)}, /*index=5*/f32[400]{0:T(5...) fusion(bf16[4,15,38,400]{3,2,1,0:T(8,128)(2,1)} %copy-done.4, ...), kind=kLoop, calls=%fused_computation.486 | loop fusion | flops 39314400 | bytes 28305344 | tf_op jit(solution)/shard_map/reduce_sum | solution.py:50
  654.7 13.3 fusion.192
  681.9 12.6 collective-permute-done.15
  698.5 25.1 %convert_reduce_fusion.4 = (f32[400]{0:T(512)}, bf16[4,12,32,400]{3,2,1,0:T(8,128)(2,1)S(1)}) fusion(bf16[4,15,38,400]{3,2,1,0:T(8,128)(2,1)S(1)} %get-tuple-element.433, f32[400]{0:T(512)S(1)} %bitcast.605, f32[400]{0:T(512)S(1)} %bitcast.604, f32[400]{0:T(512)S(1)} %bitcast.603, f32[400]{0:T(512)S(1)} %bitcast.602, f32[400]{0:T(512)S(1)} %bitcast.601, ...), kind=kLoop, calls=%fused_computation.567 | loop fusion | flops 104447600 | bytes 55612544 | tf_op jit(solution)/shard_map/reduce_sum | solution.py:270
  764.3 39.1 %all-reduce.3 = (f32[800]{0:T(1024)S(1)}, f32[800]{0:T(1024)S(1)}) all-reduce(f32[800]{0:T(1024)S(1)} %multiply_reduce_fusion.5, f32[800]{0:T(1024)S(1)} %get-tuple-element.691), channel_id=1, replica_groups=mesh['lat'=4,'lon'=8] {'lat','lon'}, use_global_device_ids=true, to_apply=%region_26.0 | all-reduce | flops 1600 | bytes 12800 | tf_op jit(solution)/shard_map/psum | solution.py:121
  863.8 14.2 reshape.631
  957.2 87.2 %dynamic-update-slice.4 = f32[8480000]{0:T(1024)} dynamic-update-slice(f32[8480000]{0:T(1024)} %dynamic-update-slice.3, f32[2560000]{0:T(1024)} %reshape.630, s32[]{} %constant.210) | dynamic-update-slice | bytes 20480004
  1044.4 87.0 %dynamic-update-slice.5 = f32[8480000]{0:T(1024)} dynamic-update-slice(f32[8480000]{0:T(1024)} %dynamic-update-slice.4, f32[2560000]{0:T(1024)} %reshape.631, s32[]{} %constant.211) | dynamic-update-slice | bytes 20480004
  1131.4 17.6 dynamic-update-slice.6
  1149.0 21.8 dynamic-update-slice.7
  1170.7 22.7 dynamic-update-slice.8
  1199.4 553.5 %all-reduce.15 = (bf16[8480000]{0:T(1024)(128)(2,1)}, f32[400]{0:T(512)S(1)}, f32[400]{0:T(512)S(1)}) all-reduce(f32[8480000]{0:T(1024)} %dynamic-update-slice.8, f32[400]{0:T(512)S(1)} %multiply_reduce_fusion.2, f32[400]{0:T(512)S(1)} %get-tuple-element.693), channel_id=2, replica_groups=mesh['lat'=4,'lon'=8] {'lat','lon'}, use_global_device_ids=true, to_apply=%region_187.0.clone | all-reduce | flops 8480800 | bytes 50886400
  1824.1 94.5 %all-reduce.12.cloned.1.call-done = f32[87600]{0:T(1024)} async-done(((f32[87600]{0:T(1024)}), f32[87600]{0:T(1024)}) %all-reduce.12.cloned.1.call-update) | async-done | bytes 350416 | tf_op jit(solution)/shard_map/psum | solution.py:325
  1932.7 25.4 %fusion.269 = bf16[4,12,32,400]{3,2,1,0:T(8,128)(2,1)} fusion(f32[4,12,32,400]{3,0,2,1:T(4,128)S(1)} %bitcast.451, bf16[4,12,32,400]{3,2,1,0:T(8,128)(2,1)S(1)} %copy-done.17, bf16[4,12,3,400]{3,2,1,0:T(4,128)(2,1)S(1)} %collective-permute-done.21, bf16[4,12,3,400]{3,2,1,0:T(4,128)(2,1)S(1)} %collective-permute-done.20, ...), kind=kLoop, calls=%fused_computation.563 | loop fusion | flops 102604800 | bytes 56839744 | tf_op jit(solution)/shard_map/convert_element_type | solution.py:293
  1958.1 249.6 %all-reduce.14.cloned.1.call-done = bf16[8480000]{0:T(1024)(128)(2,1)} async-done(((bf16[8480000]{0:T(1024)(128)(2,1)}), bf16[8480000]{0:T(1024)(128)(2,1)}) %all-reduce.14.cloned.1.call-update) | async-done | bytes 16960016
  2218.5 13.5 slice.3016
  2232.0 12.2 copy.181
  (1029 shorter events, 588.1 us)
Async XLA Ops:
  7.2 191.1 %all-gather.19.cloned.1.call-start = ((), (), s32[]{:S(2)}) async-start(), calls=%async_computation.6 | async-start | bytes 1730560 | tf_op jit(solution)/shard_map/all_gather | solution.py:189
  8.0 222.9 %all-gather.11.cloned.1.call-start = ((), (), s32[]{:S(2)}) async-start(), calls=%async_computation | async-start | bytes 2048000 | tf_op jit(solution)/shard_map/all_gather | solution.py:190
  8.7 344.4 %all-gather.13.cloned.1.call-start = ((), (), s32[]{:S(2)}) async-start(), calls=%async_computation.1 | async-start | bytes 6400000 | tf_op jit(solution)/shard_map/all_gather | solution.py:192
  9.4 360.1 %all-gather.15.cloned.1.call-start = ((), (), s32[]{:S(2)}) async-start(), calls=%async_computation.2 | async-start | bytes 7168000 | tf_op jit(solution)/shard_map/all_gather | solution.py:193
  10.0 388.8 %all-gather.21.cloned.1.call-start = ((), (), s32[]{:S(2)}) async-start(), calls=%async_computation.7 | async-start | bytes 1730560 | tf_op jit(solution)/shard_map/all_gather | solution.py:195
  10.6 512.3 %all-gather.17.cloned.1.call-start = ((), (), s32[]{:S(2)}) async-start(), calls=%async_computation.3 | async-start | bytes 2048000 | tf_op jit(solution)/shard_map/all_gather | solution.py:196
  11.6 57.0 %collective-permute-start = (bf16[4,12,3,400]{3,2,1,0:T(4,128)(2,1)}, bf16[4,12,3,400]{3,2,1,0:T(4,128)(2,1)}, u32[]{:S(2)}, u32[]{:S(2)}) collective-permute-start(bf16[4,12,3,400]{3,2,1,0:T(4,128)(2,1)} %get-tuple-element.451), channel_id=1, source_target_pairs={{0,1},{1,2},{2,3},{3,4},{4,5},{5,6},{6,7},{7,0},{8,9},{9,10},{10,1... | collective-permute-start | bytes 345608 | tf_op jit(solution)/shard_map/ppermute | solution.py:17
  12.0 56.6 %collective-permute-start.1 = (bf16[4,12,3,400]{3,2,1,0:T(4,128)(2,1)}, bf16[4,12,3,400]{3,2,1,0:T(4,128)(2,1)}, u32[]{:S(2)}, u32[]{:S(2)}) collective-permute-start(bf16[4,12,3,400]{3,2,1,0:T(4,128)(2,1)} %get-tuple-element.452), channel_id=1, source_target_pairs={{1,0},{2,1},{3,2},{4,3},{5,4},{6,5},{7,6},{0,7},{9,8},{10,9},{11,1... | collective-permute-start | bytes 345608 | tf_op jit(solution)/shard_map/ppermute | solution.py:20
  16.1 1902.5 %all-reduce.12.cloned.1.call-start = ((), (), s32[]{:S(2)}) async-start(), calls=%async_computation.4 | async-start | bytes 704512 | tf_op jit(solution)/shard_map/psum | solution.py:325
  70.9 50.0 %collective-permute-start.2 = (bf16[4,3,38,400]{3,2,1,0:T(8,128)(2,1)}, bf16[4,3,38,400]{3,2,1,0:T(8,128)(2,1)}, u32[]{:S(2)}, u32[]{:S(2)}) collective-permute-start(bf16[4,3,38,400]{3,2,1,0:T(8,128)(2,1)} %get-tuple-element.442), channel_id=1, source_target_pairs={{0,8},{8,16},{16,24},{1,9},{9,17},{17,25},{2,10},{10,18},{18,26},{... | collective-permute-start | bytes 1094408 | tf_op jit(solution)/shard_map/ppermute | solution.py:17
  73.8 47.1 %collective-permute-start.3 = (bf16[4,3,38,400]{3,2,1,0:T(8,128)(2,1)}, bf16[4,3,38,400]{3,2,1,0:T(8,128)(2,1)}, u32[]{:S(2)}, u32[]{:S(2)}) collective-permute-start(bf16[4,3,38,400]{3,2,1,0:T(8,128)(2,1)} %get-tuple-element.443), channel_id=1, source_target_pairs={{8,0},{16,8},{24,16},{9,1},{17,9},{25,17},{10,2},{18,10},{26,18},{... | collective-permute-start | bytes 1094408 | tf_op jit(solution)/shard_map/ppermute | solution.py:20
  253.8 7.9 collective-permute-start.4
  253.9 7.8 collective-permute-start.5
  262.8 18.9 collective-permute-start.6
  266.6 33.1 %collective-permute-start.7 = (bf16[4,3,22,800]{3,2,1,0:T(8,128)(2,1)S(1)}, bf16[4,3,22,800]{3,2,1,0:T(8,128)(2,1)S(1)}, u32[]{:S(2)}, u32[]{:S(2)}) collective-permute-start(bf16[4,3,22,800]{3,2,1,0:T(8,128)(2,1)S(1)} %get-tuple-element.460), channel_id=1, source_target_pairs={{8,0},{16,8},{24,16},{9,1},{17,9},{25,17},{10,2},{18,10},{26,18},{... | collective-permute-start | bytes 1267208 | tf_op jit(solution)/shard_map/ppermute | solution.py:20
  383.7 8.3 collective-permute-start.8
  383.8 8.3 collective-permute-start.9
  392.6 15.1 collective-permute-start.10
  396.8 23.6 %collective-permute-start.11 = (bf16[4,3,38,400]{3,2,1,0:T(8,128)(2,1)S(1)}, bf16[4,3,38,400]{3,2,1,0:T(8,128)(2,1)}, u32[]{:S(2)}, u32[]{:S(2)}) collective-permute-start(bf16[4,3,38,400]{3,2,1,0:T(8,128)(2,1)S(1)} %get-tuple-element.439), channel_id=1, source_target_pairs={{8,0},{16,8},{24,16},{9,1},{17,9},{25,17},{10,2},{18,10},{26,18},{... | collective-permute-start | bytes 1094408 | tf_op jit(solution)/shard_map/ppermute | solution.py:20
  626.7 41.5 %collective-permute-start.12 = (bf16[4,12,3,400]{3,2,1,0:T(4,128)(2,1)}, bf16[4,12,3,400]{3,2,1,0:T(4,128)(2,1)S(1)}, u32[]{:S(2)}, u32[]{:S(2)}) collective-permute-start(bf16[4,12,3,400]{3,2,1,0:T(4,128)(2,1)} %get-tuple-element.447), channel_id=1, source_target_pairs={{0,1},{1,2},{2,3},{3,4},{4,5},{5,6},{6,7},{7,0},{8,9},{9,10},{10,1... | collective-permute-start | bytes 345608 | tf_op jit(solution)/shard_map/ppermute | solution.py:17
  626.7 41.5 %collective-permute-start.13 = (bf16[4,12,3,400]{3,2,1,0:T(4,128)(2,1)}, bf16[4,12,3,400]{3,2,1,0:T(4,128)(2,1)}, u32[]{:S(2)}, u32[]{:S(2)}) collective-permute-start(bf16[4,12,3,400]{3,2,1,0:T(4,128)(2,1)} %get-tuple-element.448), channel_id=1, source_target_pairs={{1,0},{2,1},{3,2},{4,3},{5,4},{6,5},{7,6},{0,7},{9,8},{10,9},{11,1... | collective-permute-start | bytes 345608 | tf_op jit(solution)/shard_map/ppermute | solution.py:20
  670.1 11.8 collective-permute-start.14
  674.3 20.2 collective-permute-start.15
  828.1 9.8 collective-permute-start.16
  828.1 9.8 collective-permute-start.17
  839.5 39.3 %collective-permute-start.18 = (bf16[4,3,22,800]{3,2,1,0:T(8,128)(2,1)}, bf16[4,3,22,800]{3,2,1,0:T(8,128)(2,1)S(1)}, u32[]{:S(2)}, u32[]{:S(2)}) collective-permute-start(bf16[4,3,22,800]{3,2,1,0:T(8,128)(2,1)} %get-tuple-element.455), channel_id=1, source_target_pairs={{0,8},{8,16},{16,24},{1,9},{9,17},{17,25},{2,10},{10,18},{18,26},{... | collective-permute-start | bytes 1267208 | tf_op jit(solution)/shard_map/ppermute | solution.py:17
  843.8 35.1 %collective-permute-start.19 = (bf16[4,3,22,800]{3,2,1,0:T(8,128)(2,1)}, bf16[4,3,22,800]{3,2,1,0:T(8,128)(2,1)}, u32[]{:S(2)}, u32[]{:S(2)}) collective-permute-start(bf16[4,3,22,800]{3,2,1,0:T(8,128)(2,1)} %get-tuple-element.456), channel_id=1, source_target_pairs={{8,0},{16,8},{24,16},{9,1},{17,9},{25,17},{10,2},{18,10},{26,18},{... | collective-permute-start | bytes 1267208 | tf_op jit(solution)/shard_map/ppermute | solution.py:20
  1790.6 417.0 %all-reduce.14.cloned.1.call-start = ((), (), s32[]{:S(2)}) async-start(), calls=%async_computation.5 | async-start | bytes 33923072
  1808.6 9.2 collective-permute-start.20
  1808.7 9.2 collective-permute-start.21
  1818.4 110.0 %collective-permute-start.22 = (bf16[4,3,38,400]{3,2,1,0:T(8,128)(2,1)S(1)}, bf16[4,3,38,400]{3,2,1,0:T(8,128)(2,1)}, u32[]{:S(2)}, u32[]{:S(2)}) collective-permute-start(bf16[4,3,38,400]{3,2,1,0:T(8,128)(2,1)S(1)} %get-tuple-element.430), channel_id=1, source_target_pairs={{0,8},{8,16},{16,24},{1,9},{9,17},{17,25},{2,10},{10,18},{18,26},{... | collective-permute-start | bytes 1094408 | tf_op jit(solution)/shard_map/ppermute | solution.py:17
  1822.8 105.6 %collective-permute-start.23 = (bf16[4,3,38,400]{3,2,1,0:T(8,128)(2,1)S(1)}, bf16[4,3,38,400]{3,2,1,0:T(8,128)(2,1)}, u32[]{:S(2)}, u32[]{:S(2)}) collective-permute-start(bf16[4,3,38,400]{3,2,1,0:T(8,128)(2,1)S(1)} %get-tuple-element.431), channel_id=1, source_target_pairs={{8,0},{16,8},{24,16},{9,1},{17,9},{25,17},{10,2},{18,10},{26,18},{... | collective-permute-start | bytes 1094408 | tf_op jit(solution)/shard_map/ppermute | solution.py:20
  (341 other events, 7701.7 us)
Sparse Core Ops, SparseCore 0:
  9.9 34.9 all-gather.18
  46.7 43.4 all-gather.10
  92.1 60.4 all-gather.12
  154.3 66.2 all-gather.14
  222.3 29.3 all-gather.20
  253.4 41.3 all-gather.16
  1790.8 127.8 all-reduce.11
  1926.0 281.6 all-reduce.13
where the time goes:
time: 2330 us; the launch traced here: 2300 us
  blocking collectives  791 us (34%)
  local copies, waits for them, and re-layouts  543 us (23%)
  waiting for transfers between devices  415 us (18%)
  other arithmetic  286 us (12%)
  matrix products  192 us (8%)
  starting transfers between devices  54.6 us (2%)
    unnamed x1, blocking collectives  554 us
    unnamed x720, local copies, waits for them, and re-layouts  288 us
    unnamed x9, waiting for transfers between devices  253 us
    psum x3, blocking collectives, block_forward(): lax.psum((local_sums[0], local_sums[1], local_sums[2]), ('lat', 'lon'))  121 us
    psum x1, waiting for transfers between devices, shards(): small_total = lax.psum(small_vector, ('lat', 'lon'))  94.5 us
    reduce_sum x11, other arithmetic, kernel_terms(): row_terms.append(jnp.sum(window * upstream, axis=(0, 1, 2)))  88.1 us
    psum x2, blocking collectives, block_backward(): lax.psum((local_back[0], local_back[1]), ('lat', 'lon'))  80.2 us
    dot_general x3, matrix products, block_forward(): jnp.dot(normed, up_weight, preferred_element_type=jnp.float32)  76 us
  transfers between devices with their start and end apart: 32, of which 10 were waited for; matrix products, arithmetic and copies ran while one was open for 18% of the time, Pallas kernels for 0%

commit v1 on v0

--- a/solution.py
+++ b/solution.py
@@ -118,7 +118,7 @@
         jnp.sum(grad_normed, axis=(0, 1, 2)),
         jnp.sum(grad_normed * unit_norm, axis=(0, 1, 2)),
     )
-    grad_shift, grad_gain = lax.psum((local_back[0], local_back[1]), ("lat", "lon"))
+    grad_shift, grad_gain = jax.lax.psum(jax.lax.psum((local_back[0], local_back[1]), "lon"), "lat")
     gain_float = scale_gain.astype(jnp.float32)
     grad_mixed = norm_factor * (
         gain_float * grad_normed

time: 2330 us -> 2200 us (0.944)
  waiting for transfers between devices: 415 us -> 301 us
    psum x1, waiting for transfers between devices: 94.5 us -> 0.02 us  [shards(): small_total = lax.psum(small_vector, ('lat', 'lon'))]
    unnamed x9, waiting for transfers between devices: 253 us -> 209 us
    ppermute x12, waiting for transfers between devices: 43.3 us -> 67.2 us  [padded(): lax.ppermute(lax.slice_in_dim(block, 0, width, axis=dim), axis, backward)]
    psum x2 -> x6, blocking collectives: 80.2 us -> 68.5 us  [the longest x3 41.4 us: block_backward(): jax.lax.psum((local_back[0], local_back[1]), 'lon')]
    unnamed x720 -> x756, local copies, waits for them, and re-layouts: 288 us -> 287 us
  transfers between devices with their start and end apart: 32 -> 32, of which waited for: 10 -> 14; matrix products, arithmetic and copies ran while one was open for 18% -> 32% of each run, Pallas kernels for 0% -> 0%
where the time goes in v1:
time: 2200 us; the launch traced here: 2170 us
  blocking collectives  776 us (35%)
  local copies, waits for them, and re-layouts  547 us (25%)
  waiting for transfers between devices  301 us (14%)
  other arithmetic  288 us (13%)
  matrix products  196 us (9%)
  starting transfers between devices  42.3 us (2%)
    unnamed x1, blocking collectives  550 us
    unnamed x756, local copies, waits for them, and re-layouts  287 us
    unnamed x9, waiting for transfers between devices  209 us
    psum x3, blocking collectives, block_forward(): lax.psum((local_sums[0], local_sums[1], local_sums[2]), ('lat', 'lon'))  126 us
    reduce_sum x11, other arithmetic, kernel_terms(): row_terms.append(jnp.sum(window * upstream, axis=(0, 1, 2)))  90.4 us
    dot_general x3, matrix products, block_forward(): jnp.dot(normed, up_weight, preferred_element_type=jnp.float32)  76 us
    slice x18, local copies, waits for them, and re-layouts, unpack(): pieces.append(vector[offset:offset + length].reshape(extent))  71.3 us
    ppermute x12, waiting for transfers between devices, padded(): lax.ppermute(lax.slice_in_dim(block, 0, width, axis=dim), axis, backward)  67.2 us
  transfers between devices with their start and end apart: 32, of which 14 were waited for; matrix products, arithmetic and copies ran while one was open for 32% of the time, Pallas kernels for 0%

profile of v1, /device:TPU:0, one launch (start us, length us, event | category | flops | bytes accessed | tf_op | source)
XLA Modules:
  0.0 2171.9 jit_solution(7235238373120811850)
XLA Ops:
  35.9 17.0 all-gather.1
  55.0 14.5 all-gather.2
  124.2 25.7 %multiply_reduce_fusion.1 = (f32[400]{0:T(512)}, f32[400]{0:T(512)}, f32[4,12,32,400]{3,2,1,0:T(8,128)}) fusion(f32[4,12,32]{2,1,0:T(8,128)S(1)} %copy-done.49, bf16[4,15,38,400]{3,2,1,0:T(8,128)(2,1)S(1)} %get-tuple-element.446, f32[400]{0:T(512)S(1)} %bitcast.485, f32[400]{0:T(512)S(1)} %bitcast.484, f32[400]{0:T(512)S(1)} %bitcast.483, ...), kind=kLoop, calls=%fused_computation.214 | loop fusion | flops 97688800 | bytes 59185344 | tf_op jit(solution)/shard_map/reduce_sum | solution.py:77
  149.9 46.0 %all-reduce.4 = (f32[400]{0:T(512)S(1)}, f32[]{:T(128)}, f32[400]{0:T(512)S(1)}) all-reduce(f32[400]{0:T(512)} %get-tuple-element.207, f32[]{:T(128)} %convert_reduce_fusion.9, f32[400]{0:T(512)} %get-tuple-element.206), channel_id=1, replica_groups=mesh['lat'=4,'lon'=8] {'lat','lon'}, use_global_device_ids=true, to_apply=%region_5.0 | all-reduce | flops 801 | bytes 6408 | tf_op jit(solution)/shard_map/psum | solution.py:81
  202.1 29.4 %multiply_convert_fusion.1 = (bf16[1536,1600]{0,1:T(8,128)(2,1)}, f32[1536,1600]{0,1:T(8,128)}, f32[1536,1600]{0,1:T(8,128)}) fusion(f32[1600]{0:T(1024)S(1)} %copy-done.335, bf16[1536,400]{1,0:T(8,128)(2,1)S(1)} %bitcast.461, bf16[400,1600]{1,0:T(8,128)(2,1)} %reshape.643), kind=kOutput, calls=%fused_computation.171 | convolution fusion | flops 2128281600 | bytes 27091200 | tf_op jit(solution)/shard_map/dot_general | solution.py:92
  270.8 14.0 collective-permute-done.6
  284.8 12.9 collective-permute-done.7
  311.1 39.8 %all-reduce.3 = (f32[800]{0:T(1024)S(1)}, f32[]{:T(128)}, f32[800]{0:T(1024)S(1)}) all-reduce(f32[800]{0:T(1024)S(1)} %get-tuple-element.279, f32[]{:T(128)} %reduce_sum.1550, f32[800]{0:T(1024)S(1)} %get-tuple-element.278), channel_id=1, replica_groups=mesh['lat'=4,'lon'=8] {'lat','lon'}, use_global_device_ids=true, to_apply=%region_13.0 | all-reduce | flops 1601 | bytes 12808 | tf_op jit(solution)/shard_map/psum | solution.py:81
  351.9 16.4 multiply_convert_fusion.2
  404.9 12.4 collective-permute-done.11
  421.9 24.7 %multiply_reduce_fusion = (f32[400]{0:T(512)S(1)}, f32[400]{0:T(512)S(1)}, f32[4,12,32,400]{3,2,1,0:T(8,128)}) fusion(f32[4,12,32]{2,1,0:T(8,128)S(1)} %copy-done.51, bf16[4,15,38,400]{3,2,1,0:T(8,128)(2,1)S(1)} %get-tuple-element.442, f32[400]{0:T(512)S(1)} %bitcast.594, f32[400]{0:T(512)S(1)} %bitcast.593, f32[400]{0:T(512)S(1)} %bitcast.592, ...), kind=kLoop, calls=%fused_computation.212 | loop fusion | flops 103218400 | bytes 55614144 | tf_op jit(solution)/shard_map/reduce_sum | solution.py:77
  446.7 39.8 %all-reduce.2 = (f32[400]{0:T(512)S(1)}, f32[400]{0:T(512)S(1)}) all-reduce(f32[400]{0:T(512)S(1)} %get-tuple-element.205, f32[400]{0:T(512)S(1)} %get-tuple-element.204), channel_id=1, replica_groups=mesh['lat'=4,'lon'=8] {'lat','lon'}, use_global_device_ids=true, to_apply=%region_17.0 | all-reduce | flops 800 | bytes 6400 | tf_op jit(solution)/shard_map/psum | solution.py:81
  490.9 30.1 %multiply_convert_fusion = (bf16[1536,1600]{0,1:T(8,128)(2,1)}, f32[1536,1600]{0,1:T(8,128)}, f32[1536,1600]{0,1:T(8,128)}) fusion(f32[1600]{0:T(1024)S(1)} %copy-done.334, bf16[1536,400]{1,0:T(8,128)(2,1)S(1)} %bitcast.463, bf16[400,1600]{1,0:T(8,128)(2,1)S(1)} %copy-done.60), kind=kOutput, calls=%fused_computation.158 | convolution fusion | flops 2128281600 | bytes 27091200 | tf_op jit(solution)/shard_map/dot_general | solution.py:92
  544.0 13.9 all-reduce.7
  568.5 22.6 %fusion.193 = (f32[400]{0:T(512)S(1)}, f32[400]{0:T(512)S(1)}, f32[400]{0:T(512)S(1)}, f32[400]{0:T(512)S(1)}, f32[400]{0:T(512)S(1)}, /*index=5*/f32[400]{0:T(5...) fusion(bf16[4,15,38,400]{3,2,1,0:T(8,128)(2,1)} %copy-done.4, ...), kind=kLoop, calls=%fused_computation.486 | loop fusion | flops 39314400 | bytes 28305344 | tf_op jit(solution)/shard_map/reduce_sum | solution.py:50
  615.8 13.8 fusion.192
  665.0 25.0 %convert_reduce_fusion.4 = (f32[400]{0:T(512)}, bf16[4,12,32,400]{3,2,1,0:T(8,128)(2,1)S(1)}) fusion(bf16[4,15,38,400]{3,2,1,0:T(8,128)(2,1)S(1)} %get-tuple-element.438, f32[400]{0:T(512)} %bitcast.643, f32[400]{0:T(512)} %bitcast.642, f32[400]{0:T(512)} %bitcast.641, f32[400]{0:T(512)} %bitcast.640, f32[400]{0:T(512)} %bitcast.639, f32[400]{0:T(512)} %bitcast.638, ...), kind=kLoop, calls=%fused_computation.567 | loop fusion | flops 104447600 | bytes 55612544 | tf_op jit(solution)/shard_map/reduce_sum | solution.py:270
  718.8 13.9 all-reduce.6
  805.4 14.1 reshape.631
  837.2 12.8 collective-permute-done.19
  875.4 12.6 convert_reduce_fusion.1
  909.9 13.6 all-reduce.5
  995.3 87.2 %dynamic-update-slice.4 = f32[8480000]{0:T(1024)} dynamic-update-slice(f32[8480000]{0:T(1024)} %dynamic-update-slice.3, f32[2560000]{0:T(1024)} %reshape.630, s32[]{} %constant.210) | dynamic-update-slice | bytes 20480004
  1082.5 87.0 %dynamic-update-slice.5 = f32[8480000]{0:T(1024)} dynamic-update-slice(f32[8480000]{0:T(1024)} %dynamic-update-slice.4, f32[2560000]{0:T(1024)} %reshape.631, s32[]{} %constant.211) | dynamic-update-slice | bytes 20480004
  1169.5 17.6 dynamic-update-slice.6
  1187.1 21.8 %dynamic-update-slice.7 = f32[8480000]{0:T(1024)} dynamic-update-slice(f32[8480000]{0:T(1024)} %dynamic-update-slice.6, f32[640000]{0:T(1024)S(1)} %copy-done.29, s32[]{} %constant.213) | dynamic-update-slice | bytes 5120004
  1208.8 22.7 %dynamic-update-slice.8 = f32[8480000]{0:T(1024)} dynamic-update-slice(f32[8480000]{0:T(1024)} %dynamic-update-slice.7, f32[640000]{0:T(1024)} %reshape.637, s32[]{} %constant.214) | dynamic-update-slice | bytes 5120004 | tf_op jit(solution)/shard_map/concatenate | solution.py:305
  1231.5 550.5 %all-reduce.18 = bf16[8480000]{0:T(1024)(128)(2,1)} all-reduce(f32[8480000]{0:T(1024)} %dynamic-update-slice.8), channel_id=2, replica_groups=mesh['lat'=4,'lon'=8] {'lat','lon'}, use_global_device_ids=true, to_apply=%region_193.0.clone | all-reduce | flops 8480000 | bytes 50880000
  1831.9 12.6 collective-permute-done.23
  1848.5 25.4 %fusion.269 = bf16[4,12,32,400]{3,2,1,0:T(8,128)(2,1)} fusion(f32[4,12,32,400]{3,0,2,1:T(4,128)S(1)} %bitcast.451, bf16[4,12,32,400]{3,2,1,0:T(8,128)(2,1)S(1)} %copy-done.17, bf16[4,12,3,400]{3,2,1,0:T(4,128)(2,1)S(1)} %collective-permute-done.21, bf16[4,12,3,400]{3,2,1,0:T(4,128)(2,1)S(1)} %collective-permute-done.20, ...), kind=kLoop, calls=%fused_computation.563 | loop fusion | flops 102604800 | bytes 56839744 | tf_op jit(solution)/shard_map/convert_element_type | solution.py:293
  1873.9 206.2 %all-reduce.17.cloned.1.call-done = bf16[8480000]{0:T(1024)(128)(2,1)} async-done(((bf16[8480000]{0:T(1024)(128)(2,1)}), bf16[8480000]{0:T(1024)(128)(2,1)}) %all-reduce.17.cloned.1.call-update) | async-done | bytes 16960016
  2121.1 13.7 slice.3016
  (1070 shorter events, 641.5 us)
Async XLA Ops:
  7.2 191.9 %all-gather.19.cloned.1.call-start = ((), (), s32[]{:S(2)}) async-start(), calls=%async_computation.6 | async-start | bytes 1730560 | tf_op jit(solution)/shard_map/all_gather | solution.py:189
  8.0 223.6 %all-gather.11.cloned.1.call-start = ((), (), s32[]{:S(2)}) async-start(), calls=%async_computation | async-start | bytes 2048000 | tf_op jit(solution)/shard_map/all_gather | solution.py:190
  8.7 343.1 %all-gather.13.cloned.1.call-start = ((), (), s32[]{:S(2)}) async-start(), calls=%async_computation.1 | async-start | bytes 6400000 | tf_op jit(solution)/shard_map/all_gather | solution.py:192
  9.4 358.9 %all-gather.15.cloned.1.call-start = ((), (), s32[]{:S(2)}) async-start(), calls=%async_computation.2 | async-start | bytes 7168000 | tf_op jit(solution)/shard_map/all_gather | solution.py:193
  10.0 388.9 %all-gather.21.cloned.1.call-start = ((), (), s32[]{:S(2)}) async-start(), calls=%async_computation.7 | async-start | bytes 1730560 | tf_op jit(solution)/shard_map/all_gather | solution.py:195
  10.6 510.4 %all-gather.17.cloned.1.call-start = ((), (), s32[]{:S(2)}) async-start(), calls=%async_computation.3 | async-start | bytes 2048000 | tf_op jit(solution)/shard_map/all_gather | solution.py:196
  11.6 58.0 %collective-permute-start.1 = (bf16[4,12,3,400]{3,2,1,0:T(4,128)(2,1)}, bf16[4,12,3,400]{3,2,1,0:T(4,128)(2,1)}, u32[]{:S(2)}, u32[]{:S(2)}) collective-permute-start(bf16[4,12,3,400]{3,2,1,0:T(4,128)(2,1)} %get-tuple-element.457), channel_id=1, source_target_pairs={{1,0},{2,1},{3,2},{4,3},{5,4},{6,5},{7,6},{0,7},{9,8},{10,9},{11,1... | collective-permute-start | bytes 345608 | tf_op jit(solution)/shard_map/ppermute | solution.py:20
  16.1 53.5 %collective-permute-start = (bf16[4,12,3,400]{3,2,1,0:T(4,128)(2,1)}, bf16[4,12,3,400]{3,2,1,0:T(4,128)(2,1)}, u32[]{:S(2)}, u32[]{:S(2)}) collective-permute-start(bf16[4,12,3,400]{3,2,1,0:T(4,128)(2,1)} %get-tuple-element.456), channel_id=1, source_target_pairs={{0,1},{1,2},{2,3},{3,4},{4,5},{5,6},{6,7},{7,0},{8,9},{9,10},{10,1... | collective-permute-start | bytes 345608 | tf_op jit(solution)/shard_map/ppermute | solution.py:17
  16.1 1801.8 %all-reduce.15.cloned.1.call-start = ((), (), s32[]{:S(2)}) async-start(), calls=%async_computation.4 | async-start | bytes 704512 | tf_op jit(solution)/shard_map/psum | solution.py:325
  71.9 47.6 %collective-permute-start.2 = (bf16[4,3,38,400]{3,2,1,0:T(8,128)(2,1)}, bf16[4,3,38,400]{3,2,1,0:T(8,128)(2,1)}, u32[]{:S(2)}, u32[]{:S(2)}) collective-permute-start(bf16[4,3,38,400]{3,2,1,0:T(8,128)(2,1)} %get-tuple-element.447), channel_id=1, source_target_pairs={{0,8},{8,16},{16,24},{1,9},{9,17},{17,25},{2,10},{10,18},{18,26},{... | collective-permute-start | bytes 1094408 | tf_op jit(solution)/shard_map/ppermute | solution.py:17
  74.9 44.6 %collective-permute-start.3 = (bf16[4,3,38,400]{3,2,1,0:T(8,128)(2,1)}, bf16[4,3,38,400]{3,2,1,0:T(8,128)(2,1)}, u32[]{:S(2)}, u32[]{:S(2)}) collective-permute-start(bf16[4,3,38,400]{3,2,1,0:T(8,128)(2,1)} %get-tuple-element.448), channel_id=1, source_target_pairs={{8,0},{16,8},{24,16},{9,1},{17,9},{25,17},{10,2},{18,10},{26,18},{... | collective-permute-start | bytes 1094408 | tf_op jit(solution)/shard_map/ppermute | solution.py:20
  254.3 5.9 collective-permute-start.5
  256.5 6.6 collective-permute-start.4
  264.2 20.6 collective-permute-start.6
  267.2 30.5 %collective-permute-start.7 = (bf16[4,3,22,800]{3,2,1,0:T(8,128)(2,1)S(1)}, bf16[4,3,22,800]{3,2,1,0:T(8,128)(2,1)S(1)}, u32[]{:S(2)}, u32[]{:S(2)}) collective-permute-start(bf16[4,3,22,800]{3,2,1,0:T(8,128)(2,1)S(1)} %get-tuple-element.465), channel_id=1, source_target_pairs={{8,0},{16,8},{24,16},{9,1},{17,9},{25,17},{10,2},{18,10},{26,18},{... | collective-permute-start | bytes 1267208 | tf_op jit(solution)/shard_map/ppermute | solution.py:20
  382.5 6.1 collective-permute-start.9
  383.6 7.8 collective-permute-start.8
  392.0 13.0 collective-permute-start.10
  396.9 20.4 collective-permute-start.11
  615.1 19.5 collective-permute-start.13
  615.1 19.5 collective-permute-start.12
  635.2 17.1 collective-permute-start.14
  637.7 23.3 %collective-permute-start.15 = (bf16[4,3,38,400]{3,2,1,0:T(8,128)(2,1)S(1)}, bf16[4,3,38,400]{3,2,1,0:T(8,128)(2,1)}, u32[]{:S(2)}, u32[]{:S(2)}) collective-permute-start(bf16[4,3,38,400]{3,2,1,0:T(8,128)(2,1)S(1)} %get-tuple-element.440), channel_id=1, source_target_pairs={{8,0},{16,8},{24,16},{9,1},{17,9},{25,17},{10,2},{18,10},{26,18},{... | collective-permute-start | bytes 1094408 | tf_op jit(solution)/shard_map/ppermute | solution.py:20
  767.8 51.7 %collective-permute-start.17 = (bf16[4,6,3,800]{3,2,1,0:T(4,128)(2,1)}, bf16[4,6,3,800]{3,2,1,0:T(4,128)(2,1)S(1)}, u32[]{:S(2)}, u32[]{:S(2)}) collective-permute-start(bf16[4,6,3,800]{3,2,1,0:T(4,128)(2,1)} %get-tuple-element.468), channel_id=1, source_target_pairs={{1,0},{2,1},{3,2},{4,3},{5,4},{6,5},{7,6},{0,7},{9,8},{10,9},{11,1... | collective-permute-start | bytes 345608 | tf_op jit(solution)/shard_map/ppermute | solution.py:20
  767.8 51.7 %collective-permute-start.16 = (bf16[4,6,3,800]{3,2,1,0:T(4,128)(2,1)}, bf16[4,6,3,800]{3,2,1,0:T(4,128)(2,1)}, u32[]{:S(2)}, u32[]{:S(2)}) collective-permute-start(bf16[4,6,3,800]{3,2,1,0:T(4,128)(2,1)} %get-tuple-element.467), channel_id=1, source_target_pairs={{0,1},{1,2},{2,3},{3,4},{4,5},{5,6},{6,7},{7,0},{8,9},{9,10},{10,1... | collective-permute-start | bytes 345608 | tf_op jit(solution)/shard_map/ppermute | solution.py:17
  822.1 15.0 collective-permute-start.18
  826.2 23.8 %collective-permute-start.19 = (bf16[4,3,22,800]{3,2,1,0:T(8,128)(2,1)}, bf16[4,3,22,800]{3,2,1,0:T(8,128)(2,1)}, u32[]{:S(2)}, u32[]{:S(2)}) collective-permute-start(bf16[4,3,22,800]{3,2,1,0:T(8,128)(2,1)} %get-tuple-element.461), channel_id=1, source_target_pairs={{8,0},{16,8},{24,16},{9,1},{17,9},{25,17},{10,2},{18,10},{26,18},{... | collective-permute-start | bytes 1267208 | tf_op jit(solution)/shard_map/ppermute | solution.py:20
  969.5 1110.7 %all-reduce.17.cloned.1.call-start = ((), (), s32[]{:S(2)}) async-start(), calls=%async_computation.5 | async-start | bytes 33923072
  1799.9 8.5 collective-permute-start.21
  1800.7 8.8 collective-permute-start.20
  1810.0 21.9 %collective-permute-start.22 = (bf16[4,3,38,400]{3,2,1,0:T(8,128)(2,1)S(1)}, bf16[4,3,38,400]{3,2,1,0:T(8,128)(2,1)}, u32[]{:S(2)}, u32[]{:S(2)}) collective-permute-start(bf16[4,3,38,400]{3,2,1,0:T(8,128)(2,1)S(1)} %get-tuple-element.435), channel_id=1, source_target_pairs={{0,8},{8,16},{16,24},{1,9},{9,17},{17,25},{2,10},{10,18},{18,26},{... | collective-permute-start | bytes 1094408 | tf_op jit(solution)/shard_map/ppermute | solution.py:17
  1816.6 27.9 %collective-permute-start.23 = (bf16[4,3,38,400]{3,2,1,0:T(8,128)(2,1)S(1)}, bf16[4,3,38,400]{3,2,1,0:T(8,128)(2,1)}, u32[]{:S(2)}, u32[]{:S(2)}) collective-permute-start(bf16[4,3,38,400]{3,2,1,0:T(8,128)(2,1)S(1)} %get-tuple-element.436), channel_id=1, source_target_pairs={{8,0},{16,8},{24,16},{9,1},{17,9},{25,17},{10,2},{18,10},{26,18},{... | collective-permute-start | bytes 1094408 | tf_op jit(solution)/shard_map/ppermute | solution.py:20
  (359 other events, 5896.1 us)
Sparse Core Ops, SparseCore 0:
  9.9 32.2 all-gather.18
  44.0 35.4 all-gather.10
  81.3 66.9 all-gather.12
  150.0 66.4 all-gather.14
  218.2 29.4 all-gather.20
  249.4 40.3 all-gather.16
  969.6 123.7 all-reduce.14
  1798.5 281.6 all-reduce.16
